TPU v7x, 32 devices: a whole 2x2x4 slice. The times are simulated.
32 devices in a mesh: row: 4 (over y, core), col: 8 (over z, x).
Axes of the slice: x: 2, y: 2, z: 4, core: 2. Of those that a mesh axis runs over, the one named last changes fastest.
Arguments:
- objects: float32 [2, 2, 1024, 2048], P(None, None, 'row', 'col'), may hold values from -5 to 5
- probe: float32 [2, 256, 256], replicated, may hold values from -6 to 6
- prev_partial: float32 [4, 8, 2, 256, 256], P('row', 'col'), may hold values from -6 to 6
- offsets: int32 [4, 8, 1, 2], P('row', 'col'), may hold values from 0 to 128
- counts: int32 [4, 8], P('row', 'col'), may hold values from 0 to 1
- amplitudes: float32 [4, 8, 1, 256, 256], P('row', 'col'), may hold values from 1 to 2.5
Outputs:
- new_objects: float32 [2, 2, 1024, 2048], P(None, None, 'row', 'col')
- new_probe: float32 [2, 256, 256], replicated
- new_partial: float32 [4, 8, 2, 256, 256], P('row', 'col')
All inputs are finite; a program needn't handle non-finite values.
Results may differ from a plain program's by a relative error of at most 0.0003.
Values sent between devices are 32-bit elements; how exact they have to be, the bound alone decides.
A program may use at most 64 MiB of HBM per device.

v0:
```python
import functools
import math

import jax
import jax.numpy as jnp
import numpy as np
from jax import lax
from jax.experimental import pallas as pl
from jax.experimental.pallas import tpu as pltpu
from jax.sharding import PartitionSpec as P

HALO = 64
OBJ_RATE = 0.1
PROBE_RATE = 0.3
MESH = pl.DeviceIdType.MESH

STEPS = ((-1, 0), (1, 0), (0, -1), (0, 1), (-1, -1), (-1, 1), (1, -1), (1, 1))


def split(value):
    high = value.astype(jnp.bfloat16)
    low = (value - high.astype(jnp.float32)).astype(jnp.bfloat16)
    return high, low


def operator_table(n):
    index = np.arange(n)
    angle = 2.0 * np.pi * (np.outer(index, index) % n) / n
    dft = np.exp(-1j * angle) / np.sqrt(n)
    freq = np.where(index < n // 2, index, index - n).astype(np.float64)
    phase = np.exp(1j * np.pi * freq * freq / (4.0 * n))
    prop = np.conj(dft) @ (phase[:, None] * dft)
    tables = []
    for mat in (dft, prop):
        for part in (mat.real, mat.imag, -mat.imag):
            part = part.astype(np.float32)
            high = part.astype(jnp.bfloat16)
            low = (part - high.astype(np.float32)).astype(jnp.bfloat16)
            tables += [high, low]
    return np.stack(tables).reshape(2, 3, 2, n, n)


def dot(left, right):
    return jnp.dot(left, right, preferred_element_type=jnp.float32)


def cat(parts, axis):
    return jnp.concatenate(parts, axis=axis)


def sandwich(xr, xi, table, which, conj):
    re, im, neg = table.at[which, 0], table.at[which, 1], table.at[which, 2]
    if conj:
        im, neg = neg, im
    rh, rl, ih, il, nh, nl = (p[k] for p in (re, im, neg) for k in (0, 1))
    xrh, xrl = split(xr)
    xih, xil = split(xi)
    left = cat([xrh, xih, xrl, xil, xrh, xih], 1)
    tr = dot(left, cat([rh, nh, rh, nh, rl, nl], 0))
    ti = dot(left, cat([ih, rh, ih, rh, il, rl], 0))
    trh, trl = split(tr)
    tih, til = split(ti)
    right = cat([trh, tih, trl, til, trh, tih], 0)
    yr = dot(cat([rh, nh, rh, nh, rl, nl], 1), right)
    yi = dot(cat([ih, rh, ih, rh, il, rl], 1), right)
    return yr, yi


def kernel(
    rows, cols, offs, count, obj_hbm, prev_hbm, probe_hbm, probe_k_hbm, amp_hbm, table_hbm,
    out_obj, out_probe, out_part,
    obj, prev, probe, probe_piece, amp, table,
    pw, pe, ext, rw, re_,
    acc, gn, gs, gw_, ge, qn, qs, qw, qe,
    buf1, sum1, buf2, newp,
    local_sem, halo_send, halo_recv, row_send, row_recv, col_send, col_recv,
):
    tile = obj.shape[2]
    win = probe.shape[1]
    side = tile + 2 * HALO
    row, col = lax.axis_index("row"), lax.axis_index("col")

    def exists(dr, dc):
        r, c = row + dr, col + dc
        return (r >= 0) & (r < rows) & (c >= 0) & (c < cols)

    fetches = [
        pltpu.make_async_copy(src, dst, local_sem.at[k])
        for k, (src, dst) in enumerate(
            ((obj_hbm, obj), (prev_hbm, prev), (probe_k_hbm.at[row, col], probe_piece),
             (probe_hbm, probe), (table_hbm, table), (amp_hbm, amp))
        )
    ]
    for fetch in fetches:
        fetch.start()

    barrier = pltpu.get_barrier_semaphore()

    def greet(r, c):
        pl.semaphore_signal(barrier, inc=1, device_id=(r, c), device_id_type=MESH)

    for t in range(1, rows):
        greet(lax.rem(row + t, rows), col)
    for t in range(1, cols):
        greet(row, lax.rem(col + t, cols))
    for dr, dc in STEPS[4:]:
        @pl.when(exists(dr, dc))
        def _():
            greet(row + dr, col + dc)

    lane = lax.broadcasted_iota(jnp.int32, (1, 2 * HALO), 1)
    first = lane < HALO

    def swap(value):
        return pltpu.roll(value, HALO, 1)

    fetches[0].wait()
    for s in range(2):
        head_re, head_im = obj[s, 0, :, : 2 * HALO], obj[s, 1, :, : 2 * HALO]
        tail_re, tail_im = obj[s, 0, :, tile - 2 * HALO :], obj[s, 1, :, tile - 2 * HALO :]
        pw[s] = jnp.where(first, head_re, swap(head_im))
        pe[s] = jnp.where(first, swap(tail_re), tail_im)

    north, south = pl.ds(0, HALO), pl.ds(tile + HALO, HALO)
    middle = pl.ds(HALO, tile)
    low, high = pl.ds(0, HALO), pl.ds(tile - HALO, HALO)
    wide = pl.ds(0, tile)

    def halo_plan(s):
        return (
            (obj.at[s, :, low, :], ext.at[s, :, south, wide]),
            (obj.at[s, :, high, :], ext.at[s, :, north, wide]),
            (pw.at[s], re_.at[s, middle]),
            (pe.at[s], rw.at[s, middle]),
            (pw.at[s, low], re_.at[s, south]),
            (pe.at[s, low], rw.at[s, south]),
            (pw.at[s, high], re_.at[s, north]),
            (pe.at[s, high], rw.at[s, north]),
        )

    def grad_plan(s):
        return (
            (gn.at[s], qs.at[s]),
            (gs.at[s], qn.at[s]),
            (gw_.at[s, middle], qe.at[s, middle]),
            (ge.at[s, middle], qw.at[s, middle]),
            (gw_.at[s, north], qe.at[s, south]),
            (ge.at[s, north], qw.at[s, south]),
            (gw_.at[s, south], qe.at[s, north]),
            (ge.at[s, south], qw.at[s, north]),
        )

    def plan_of(phase, s):
        return halo_plan(s) if phase == 0 else grad_plan(s)

    def copies(phase, s):
        plan = plan_of(phase, s)
        return [
            (dr, dc, dst, pltpu.make_async_remote_copy(
                src_ref=src, dst_ref=dst,
                send_sem=halo_send.at[phase, s, d], recv_sem=halo_recv.at[phase, s, d],
                device_id=(row + dr, col + dc), device_id_type=MESH))
            for d, ((dr, dc), (src, dst)) in enumerate(zip(STEPS, plan))
        ]

    order = (2, 3, 4, 5, 6, 7, 0, 1)

    def send(phase, s):
        todo = copies(phase, s)
        for d in order:
            dr, dc, dst, copy = todo[d]

            @pl.when(exists(dr, dc))
            def _():
                copy.start()

    def blank(phase, s):
        for (dr, dc), (_, dst) in zip(STEPS, plan_of(phase, s)):
            @pl.when(jnp.logical_not(exists(-dr, -dc)))
            def _():
                dst[...] = jnp.zeros(dst.shape, jnp.float32)

    def arrive(phase, s):
        for dr, dc, dst, copy in copies(phase, s):
            @pl.when(exists(-dr, -dc))
            def _():
                copy.wait_recv()

    def sent(phase, s):
        for dr, dc, dst, copy in copies(phase, s):
            @pl.when(exists(dr, dc))
            def _():
                copy.wait_send()

    def row_copies(stage):
        made = []
        for t in range(1, rows):
            peer = lax.rem(row + t, rows)
            if stage == 0:
                src, dst = prev.at[peer], buf1.at[t - 1]
            else:
                src, dst = newp.at[row], newp.at[row]
            made.append(pltpu.make_async_remote_copy(
                src_ref=src, dst_ref=dst, send_sem=row_send.at[stage, t - 1],
                recv_sem=row_recv.at[stage, t - 1], device_id=(peer, col), device_id_type=MESH))
        return made

    def col_copies(stage):
        made = []
        for t in range(1, cols):
            peer = lax.rem(col + t, cols)
            if stage == 0:
                src, dst = sum1.at[peer], buf2.at[t - 1]
            else:
                src, dst = newp.at[row, col], newp.at[row, col]
            made.append(pltpu.make_async_remote_copy(
                src_ref=src, dst_ref=dst, send_sem=col_send.at[stage, t - 1],
                recv_sem=col_recv.at[stage, t - 1], device_id=(row, peer), device_id_type=MESH))
        return made

    diagonals = sum(exists(dr, dc).astype(jnp.int32) for dr, dc in STEPS[4:])
    pl.semaphore_wait(barrier, rows - 1 + cols - 1 + diagonals)

    send(0, 0)
    fetches[1].wait()
    rs_rows = row_copies(0)
    for copy in rs_rows:
        copy.start()
    send(0, 1)

    for s in range(2):
        for part in range(2):
            ext[s, part, HALO : HALO + tile, :] = obj[s, part]
        blank(0, s)
        blank(1, s)

    for copy in rs_rows:
        copy.wait_recv()
    total = prev[row]
    for t in range(1, rows):
        total = total + buf1[t - 1]
    sum1[...] = total
    rs_cols = col_copies(0)
    for copy in rs_cols:
        copy.start()

    top, left = offs[0], offs[1]

    def one_hot(shape, axis, shift):
        longer = lax.broadcasted_iota(jnp.int32, shape, axis)
        shorter = lax.broadcasted_iota(jnp.int32, shape, 1 - axis) + shift
        shorter = jnp.where(shorter < 0, shorter + side, shorter)
        return (longer == shorter).astype(jnp.float32).astype(jnp.bfloat16)

    def twice(value, axis):
        return cat([value, value], axis)

    def window(s):
        east, west = re_[s], rw[s]
        full = cat([
            ext[s, 0, :, :tile], jnp.where(first, east, swap(west)),
            ext[s, 1, :, :tile], jnp.where(first, swap(east), west),
        ], 1)
        pick_rows = one_hot((win, side), 1, top)
        pick_cols = one_hot((side, win), 0, left - HALO)
        some = dot(twice(pick_rows, 1), cat(split(full), 0))
        some = cat([some[:, :side], some[:, side:]], 0)
        some = dot(cat(split(some), 1), twice(pick_cols, 0))
        return some[:win], some[win:]

    def place(s, gre, gim):
        put_cols = one_hot((win, side), 1, left - HALO)
        put_rows = one_hot((side, win), 0, top)
        some = dot(cat(split(cat([gre, gim], 0)), 1), twice(put_cols, 0))
        some = cat([some[:win], some[win:]], 1)
        full = dot(twice(put_rows, 1), cat(split(some), 0))
        full_re, full_im = full[:, :side], full[:, side:]
        for part, value in enumerate((full_re, full_im)):
            gn[s, part] = value[:HALO, :tile]
            gs[s, part] = value[HALO + tile :, :tile]
            acc[s, part] = value[HALO : HALO + tile, :tile]
        edge_re, edge_im = full_re[:, tile:], full_im[:, tile:]
        ge[s] = jnp.where(first, edge_re, swap(edge_im))
        gw_[s] = jnp.where(first, swap(edge_re), edge_im)

    arrive(0, 0)
    for k in (3, 4):
        fetches[k].wait()
    ar, ai = window(0)
    pr, pi = probe[0], probe[1]
    vr, vi = sandwich(pr * ar - pi * ai, pr * ai + pi * ar, table, 1, False)

    for copy in rs_cols:
        copy.wait_recv()
    fetches[2].wait()
    total = sum1[col]
    for t in range(1, cols):
        total = total + buf2[t - 1]
    rate = PROBE_RATE / math.sqrt(rows * cols)
    newp[row, col] = probe_piece[...] - rate * total
    ag_cols = col_copies(1)
    for copy in ag_cols:
        copy.start()

    arrive(0, 1)
    br, bi = window(1)
    wr, wi = sandwich(vr * br - vi * bi, vr * bi + vi * br, table, 0, False)
    fetches[5].wait()
    live = jnp.where(count[0] > 0, 2.0, 0.0)
    scale = live * (1.0 - amp[...] / jnp.sqrt(wr * wr + wi * wi + 1.0))
    xr, xi = sandwich(scale * wr, scale * wi, table, 0, True)
    place(1, xr * vr + xi * vi, xi * vr - xr * vi)
    send(1, 1)

    for copy in ag_cols:
        copy.wait_recv()
    ag_rows = row_copies(1)
    for copy in ag_rows:
        copy.start()

    ur, ui = sandwich(xr * br + xi * bi, xi * br - xr * bi, table, 1, True)
    place(0, ur * pr + ui * pi, ui * pr - ur * pi)
    send(1, 0)
    out_part[0] = ur * ar + ui * ai
    out_part[1] = ui * ar - ur * ai

    def finish(s):
        arrive(1, s)
        top_strip, bottom_strip = slice(0, HALO), slice(tile - HALO, tile)
        for part in range(2):
            acc[s, part, top_strip, :] += qn[s, part]
            acc[s, part, bottom_strip, :] += qs[s, part]
        for q, near, lanes in ((qw, True, slice(0, 2 * HALO)), (qe, False, slice(tile - 2 * HALO, tile))):
            for src, dst in (
                (slice(HALO, HALO + tile), slice(0, tile)),
                (slice(0, HALO), top_strip),
                (slice(HALO + tile, side), bottom_strip),
            ):
                value = q[s, src]
                turned = swap(value)
                if near:
                    acc[s, 0, dst, lanes] += jnp.where(first, value, 0.0)
                    acc[s, 1, dst, lanes] += jnp.where(first, turned, 0.0)
                else:
                    acc[s, 0, dst, lanes] += jnp.where(first, 0.0, turned)
                    acc[s, 1, dst, lanes] += jnp.where(first, 0.0, value)
        for part in range(2):
            out_obj[s, part] = obj[s, part] - OBJ_RATE * acc[s, part]

    finish(1)
    for copy in ag_rows:
        copy.wait_recv()
    out_probe[...] = newp[...]
    finish(0)

    for s in range(2):
        sent(0, s)
        sent(1, s)
    for copy in rs_rows + rs_cols + ag_cols + ag_rows:
        copy.wait_send()


def shards(rows, cols, objects, probe, prev_partial, offsets, counts, amplitudes):
    tile = objects.shape[2]
    win = probe.shape[-1]
    side = tile + 2 * HALO
    piece = (2 * win) // (rows * cols)
    split_shape = (rows, cols, piece, win)
    table = jnp.asarray(operator_table(win))
    f32 = jnp.float32
    smem = pl.BlockSpec(memory_space=pltpu.SMEM)
    anyspace = pl.BlockSpec(memory_space=pl.ANY)
    vmem = pl.BlockSpec(memory_space=pltpu.VMEM)
    V = lambda *shape: pltpu.VMEM(shape, f32)
    strip = (2, side, 2 * HALO)
    flat = (2, 2, HALO, tile)
    dma = pltpu.SemaphoreType.DMA
    scratch = [
        V(2, 2, tile, tile), V(*split_shape), V(2, win, win), V(piece, win), V(win, win),
        pltpu.VMEM(table.shape, jnp.bfloat16),
        V(2, tile, 2 * HALO), V(2, tile, 2 * HALO), V(2, 2, side, tile), V(*strip), V(*strip),
        V(2, 2, tile, tile),
        V(*flat), V(*flat), V(*strip), V(*strip),
        V(*flat), V(*flat), V(*strip), V(*strip),
        V(max(rows - 1, 1), cols, piece, win), V(cols, piece, win),
        V(max(cols - 1, 1), piece, win), V(*split_shape),
        dma((6,)), dma((2, 2, 8)), dma((2, 2, 8)),
        dma((2, max(rows - 1, 1))), dma((2, max(rows - 1, 1))),
        dma((2, max(cols - 1, 1))), dma((2, max(cols - 1, 1))),
    ]
    new_obj, new_probe, part = pl.pallas_call(
        functools.partial(kernel, rows, cols),
        out_shape=(
            jax.ShapeDtypeStruct(objects.shape, f32),
            jax.ShapeDtypeStruct(split_shape, f32),
            jax.ShapeDtypeStruct(probe.shape, f32),
        ),
        in_specs=[smem, smem] + [anyspace] * 6,
        out_specs=(vmem, vmem, vmem),
        scratch_shapes=scratch,
        compiler_params=pltpu.CompilerParams(
            collective_id=0, has_side_effects=True, vmem_limit_bytes=56 * 2**20
        ),
    )(
        offsets.reshape(2), counts.reshape(1), objects, prev_partial.reshape(split_shape),
        probe, probe.reshape(split_shape), amplitudes.reshape(win, win), table,
    )
    return new_obj, new_probe.reshape(probe.shape), part[None, None]


def solution(mesh):
    in_specs = (
        P(None, None, "row", "col"),
        P(),
        P("row", "col", None, None, None),
        P("row", "col", None, None),
        P("row", "col"),
        P("row", "col", None, None, None),
    )
    out_specs = (P(None, None, "row", "col"), P(), P("row", "col", None, None, None))
    body = functools.partial(shards, mesh.shape["row"], mesh.shape["col"])
    return jax.shard_map(body, mesh=mesh, in_specs=in_specs, out_specs=out_specs, check_vma=False)
```

profile of v0, /device:TPU:9, one launch (start us, length us, event | category | flops | bytes accessed | tf_op | source)
XLA Modules:
  0.0 52.6 jit_solution(16322353596521018404)
XLA Ops:
  1.3 47.3 %shard_map.94 = (f32[2,2,256,256]{3,2,1,0:T(8,128)}, f32[4,8,16,256]{3,2,1,0:T(8,128)}, f32[2,256,256]{2,1,0:T(8,128)}) custom-call(s32[2]{0:T(128)} %bitcast.13, s32[1]{0:T(128)} %bitcast.7.count, f32[2,2,256,256]{3,2,1,0:T(8,128)} %obj_hbm.1, f32[4,8,16,256]{3,2,1,0:T(8,128)} %bitcast.9, f32[2,256,256]{2,1,0:T(8,128)} %probe_hbm.1, ...), custom_call_target="tpu_custom_call" | custom-call | tf_op jit(solution)/shard_map/pallas_call | solution.py:391
  48.6 0.0 copy-start.1
  48.6 0.0 copy-start
  48.6 2.4 %copy.14 = f32[2,2,256,256]{3,2,1,0:T(8,128)} copy(f32[2,2,256,256]{3,2,1,0:T(8,128)} %get-tuple-element.12) | data formatting | bytes 2097152
  51.0 0.0 copy-done.1
  51.0 0.8 %copy.15 = f32[2,256,256]{2,1,0:T(8,128)} copy(f32[2,256,256]{2,1,0:T(8,128)S(1)} %bitcast.11) | data formatting | bytes 1048576
  51.8 0.0 copy-done
  51.8 0.8 %copy.16 = f32[1,1,2,256,256]{4,3,2,1,0:T(8,128)} copy(f32[1,1,2,256,256]{4,3,2,1,0:T(8,128)S(1)} %bitcast.10) | data formatting | bytes 1048576
Async XLA Ops:
  48.6 2.4 %copy-start.1 = (f32[4,8,16,256]{3,2,1,0:T(8,128)S(1)}, f32[4,8,16,256]{3,2,1,0:T(8,128)}, u32[]{:S(2)}) copy-start(f32[4,8,16,256]{3,2,1,0:T(8,128)} %get-tuple-element.7) | copy-start | bytes 1572868
  48.6 3.2 %copy-start = (f32[2,256,256]{2,1,0:T(8,128)S(1)}, f32[2,256,256]{2,1,0:T(8,128)}, u32[]{:S(2)}) copy-start(f32[2,256,256]{2,1,0:T(8,128)} %get-tuple-element.8) | copy-start | bytes 1572868
where the time goes:
time: 52.8 us; the launch traced here: 52.6 us
  Pallas kernels  47.3 us (90%)
  local copies, waits for them, and re-layouts  3.97 us (8%)
  between operations  1.3 us (2%)
    pallas_call x1, Pallas kernels, shards(): pl.pallas_call(functools.partial(kernel, rows, cols), out_shape=(jax.Shap...  47.3 us
    unnamed x7, local copies, waits for them, and re-layouts  3.97 us

commit v1 on v0

--- a/solution.py
+++ b/solution.py
@@ -53,16 +53,17 @@
     if conj:
         im, neg = neg, im
     rh, rl, ih, il, nh, nl = (p[k] for p in (re, im, neg) for k in (0, 1))
-    xrh, xrl = split(xr)
-    xih, xil = split(xi)
-    left = cat([xrh, xih, xrl, xil, xrh, xih], 1)
-    tr = dot(left, cat([rh, nh, rh, nh, rl, nl], 0))
-    ti = dot(left, cat([ih, rh, ih, rh, il, rl], 0))
-    trh, trl = split(tr)
-    tih, til = split(ti)
+    n = xr.shape[0]
+    high, low = split(cat([xr, xi], 0))
+    left = cat([high, low, high], 1)
+    by_re = dot(left, cat([rh, rh, rl], 0))
+    by_im = dot(left, cat([ih, ih, il], 0))
+    trh, trl = split(by_re[:n] - by_im[n:])
+    tih, til = split(by_im[:n] + by_re[n:])
     right = cat([trh, tih, trl, til, trh, tih], 0)
-    yr = dot(cat([rh, nh, rh, nh, rl, nl], 1), right)
-    yi = dot(cat([ih, rh, ih, rh, il, rl], 1), right)
+    left = cat([cat([rh, nh, rh, nh, rl, nl], 1), cat([ih, rh, ih, rh, il, rl], 1)], 0)
+    both = dot(left, right)
+    yr, yi = both[:n], both[n:]
     return yr, yi
 
 
@@ -72,7 +73,7 @@
     obj, prev, probe, probe_piece, amp, table,
     pw, pe, ext, rw, re_,
     acc, gn, gs, gw_, ge, qn, qs, qw, qe,
-    buf1, sum1, buf2, newp,
+    buf1, sum1, buf2, newp, part_buf,
     local_sem, halo_send, halo_recv, row_send, row_recv, col_send, col_recv,
 ):
     tile = obj.shape[2]
@@ -321,8 +322,15 @@
     ur, ui = sandwich(xr * br + xi * bi, xi * br - xr * bi, table, 1, True)
     place(0, ur * pr + ui * pi, ui * pr - ur * pi)
     send(1, 0)
-    out_part[0] = ur * ar + ui * ai
-    out_part[1] = ui * ar - ur * ai
+    part_buf[0] = ur * ar + ui * ai
+    part_buf[1] = ui * ar - ur * ai
+    writes = [
+        pltpu.make_async_copy(src, dst, local_sem.at[6 + k])
+        for k, (src, dst) in enumerate(
+            ((part_buf, out_part), (newp, out_probe), (acc.at[1], out_obj.at[1]), (acc.at[0], out_obj.at[0]))
+        )
+    ]
+    writes[0].start()
 
     def finish(s):
         arrive(1, s)
@@ -345,19 +353,23 @@
                     acc[s, 0, dst, lanes] += jnp.where(first, 0.0, turned)
                     acc[s, 1, dst, lanes] += jnp.where(first, 0.0, value)
         for part in range(2):
-            out_obj[s, part] = obj[s, part] - OBJ_RATE * acc[s, part]
-
-    finish(1)
+            acc[s, part] = obj[s, part] - OBJ_RATE * acc[s, part]
+
     for copy in ag_rows:
         copy.wait_recv()
-    out_probe[...] = newp[...]
+    writes[1].start()
+    finish(1)
+    writes[2].start()
     finish(0)
+    writes[3].start()
 
     for s in range(2):
         sent(0, s)
         sent(1, s)
     for copy in rs_rows + rs_cols + ag_cols + ag_rows:
         copy.wait_send()
+    for write in writes:
+        write.wait()
 
 
 def shards(rows, cols, objects, probe, prev_partial, offsets, counts, amplitudes):
@@ -370,7 +382,6 @@
     f32 = jnp.float32
     smem = pl.BlockSpec(memory_space=pltpu.SMEM)
     anyspace = pl.BlockSpec(memory_space=pl.ANY)
-    vmem = pl.BlockSpec(memory_space=pltpu.VMEM)
     V = lambda *shape: pltpu.VMEM(shape, f32)
     strip = (2, side, 2 * HALO)
     flat = (2, 2, HALO, tile)
@@ -383,8 +394,8 @@
         V(*flat), V(*flat), V(*strip), V(*strip),
         V(*flat), V(*flat), V(*strip), V(*strip),
         V(max(rows - 1, 1), cols, piece, win), V(cols, piece, win),
-        V(max(cols - 1, 1), piece, win), V(*split_shape),
-        dma((6,)), dma((2, 2, 8)), dma((2, 2, 8)),
+        V(max(cols - 1, 1), piece, win), V(*split_shape), V(2, win, win),
+        dma((10,)), dma((2, 2, 8)), dma((2, 2, 8)),
         dma((2, max(rows - 1, 1))), dma((2, max(rows - 1, 1))),
         dma((2, max(cols - 1, 1))), dma((2, max(cols - 1, 1))),
     ]
@@ -396,7 +407,7 @@
             jax.ShapeDtypeStruct(probe.shape, f32),
         ),
         in_specs=[smem, smem] + [anyspace] * 6,
-        out_specs=(vmem, vmem, vmem),
+        out_specs=(anyspace,) * 3,
         scratch_shapes=scratch,
         compiler_params=pltpu.CompilerParams(
             collective_id=0, has_side_effects=True, vmem_limit_bytes=56 * 2**20

time: 52.8 us -> 53.7 us (1.017)
  Pallas kernels: 47.3 us -> 48.3 us
    pallas_call x1, Pallas kernels: 47.3 us -> 48.3 us  [shards(): pl.pallas_call(functools.partial(kernel, rows, cols), out_shape=(jax.Shap...]
where the time goes in v1:
time: 53.7 us; the launch traced here: 53.6 us
  Pallas kernels  48.3 us (90%)
  local copies, waits for them, and re-layouts  3.97 us (7%)
  between operations  1.3 us (2%)
    pallas_call x1, Pallas kernels, shards(): pl.pallas_call(functools.partial(kernel, rows, cols), out_shape=(jax.Shap...  48.3 us
    unnamed x7, local copies, waits for them, and re-layouts  3.97 us

profile of v1, /device:TPU:9, one launch (start us, length us, event | category | flops | bytes accessed | tf_op | source)
XLA Modules:
  0.0 53.6 jit_solution(8888211160118946186)
XLA Ops:
  1.3 48.3 %shard_map.94 = (f32[2,2,256,256]{3,2,1,0:T(8,128)}, f32[4,8,16,256]{3,2,1,0:T(8,128)}, f32[2,256,256]{2,1,0:T(8,128)}) custom-call(s32[2]{0:T(128)} %bitcast.13, s32[1]{0:T(128)} %bitcast.7.count, f32[2,2,256,256]{3,2,1,0:T(8,128)} %obj_hbm.1, f32[4,8,16,256]{3,2,1,0:T(8,128)} %bitcast.9, f32[2,256,256]{2,1,0:T(8,128)} %probe_hbm.1, ...), custom_call_target="tpu_custom_call" | custom-call | tf_op jit(solution)/shard_map/pallas_call | solution.py:402
  49.6 0.0 copy-start.1
  49.6 0.0 copy-start
  49.6 2.4 %copy.14 = f32[2,2,256,256]{3,2,1,0:T(8,128)} copy(f32[2,2,256,256]{3,2,1,0:T(8,128)} %get-tuple-element.12) | data formatting | bytes 2097152
  52.0 0.0 copy-done.1
  52.0 0.8 %copy.15 = f32[2,256,256]{2,1,0:T(8,128)} copy(f32[2,256,256]{2,1,0:T(8,128)S(1)} %bitcast.11) | data formatting | bytes 1048576
  52.8 0.0 copy-done
  52.8 0.8 %copy.16 = f32[1,1,2,256,256]{4,3,2,1,0:T(8,128)} copy(f32[1,1,2,256,256]{4,3,2,1,0:T(8,128)S(1)} %bitcast.10) | data formatting | bytes 1048576
Async XLA Ops:
  49.6 2.4 %copy-start.1 = (f32[4,8,16,256]{3,2,1,0:T(8,128)S(1)}, f32[4,8,16,256]{3,2,1,0:T(8,128)}, u32[]{:S(2)}) copy-start(f32[4,8,16,256]{3,2,1,0:T(8,128)} %get-tuple-element.7) | copy-start | bytes 1572868
  49.6 3.2 %copy-start = (f32[2,256,256]{2,1,0:T(8,128)S(1)}, f32[2,256,256]{2,1,0:T(8,128)}, u32[]{:S(2)}) copy-start(f32[2,256,256]{2,1,0:T(8,128)} %get-tuple-element.8) | copy-start | bytes 1572868
